TPU v7x, 128 devices: a whole 4x4x4 slice. The times are simulated.
128 devices in a mesh: rep: 16 (over z_hi, x, core), sp: 8 (over z_lo, y).
Axes of the slice: x: 4, y: 4, z: 4 (z_hi: 2, z_lo: 2; z = z_hi * 2 + z_lo), core: 2. Of those that a mesh axis runs over, the one named last changes fastest.
Arguments:
- positions: float32 [16, 3, 65536], P('rep', None, 'sp'), may hold values from -18 to 18
- velocities: float32 [16, 3, 65536], P('rep', None, 'sp'), may hold values from -6 to 6
- strength: float32 [16, 65536], P('rep', 'sp'), may hold values from 0.5 to 2
- inv_mass: float32 [16, 65536], P('rep', 'sp'), may hold values from 0.1 to 1
- tile_lists: int32 [16, 4, 512, 4], P('rep', None, 'sp'), may hold values from 0 to 127, as said below
- solute_index: int32 [16, 2048], P('rep', 'sp'), may hold values from 0 to 8191, as said below
- scatter_weight: float32 [16, 2048], P('rep', 'sp'), may hold values from 0.3 to 3
- intensity_exp: float32 [48], replicated, may hold values from 0.5 to 3
- precision: float32 [48], replicated, may hold values from 1 to 4
Outputs:
- positions_out: float32 [16, 3, 65536], P('rep', None, 'sp')
- velocities_out: float32 [16, 3, 65536], P('rep', None, 'sp')
Inputs may be any that keep to these rules, and one draw needn't show every extreme that they name: `tile_lists`: for each replica, step and local block b of a domain (numbered 0 to 63), the 4 entries are distinct extended block numbers from b to b + 64, among them b, b + 32 and b + 64. `solute_index`: within each replica and domain the 256 entries are distinct local atom numbers.
All inputs are finite; a program needn't handle non-finite values.
Results may differ from a plain program's by a relative error of at most 0.0001.
Values sent between devices are 32-bit elements; how exact they have to be, the bound alone decides.
No kernel may reach another device: no remote copies, remote signals or barrier semaphores. Data moves between devices by JAX's collectives and lax.ppermute only.
A program may use at most 128 MiB of HBM per device.

v0:
```python
import math
import jax
import jax.numpy as jnp
from jax import lax
from jax.sharding import PartitionSpec as P

M = 784
OUTER = 2
INNER = 2
TIME_STEP = 0.05
PAIR_STRENGTH = 0.2
HALF_INVERSE = 0.03125
shell_batch = 8
group_limit = 8


def extended_2(cells, sides, width):
    for axis, dim in sides:
        count = lax.axis_size(axis)
        ends = count - 1
        head = lax.slice_in_dim(cells, 0, width, axis=dim)
        tail = lax.slice_in_dim(cells, cells.shape[dim] - width, cells.shape[dim], axis=dim)
        cells = jnp.concatenate(
            [
                lax.ppermute(tail, axis, [(i, (i + 1) % count) for i in range(ends)]),
                cells,
                lax.ppermute(head, axis, [((i + 1) % count, i) for i in range(ends)]),
            ],
            axis=dim,
        )
    return cells


def directions(total_terms):
    order_index = jnp.arange(total_terms, dtype=jnp.int32)
    height = 1.0 - (2.0 * order_index.astype(jnp.float32) + 1.0) / total_terms
    radius = jnp.sqrt(1.0 - height * height)
    azimuth = (order_index * 610 % 987).astype(jnp.float32) * (2.0 * math.pi / 987.0)
    return (radius * jnp.cos(azimuth), radius * jnp.sin(azimuth), height)


def shell_values(total_shells):
    return 1.0 + 3.0 * jnp.arange(total_shells, dtype=jnp.int32).astype(jnp.float32) / total_shells


def projection(points, dir_x, dir_y, dir_z):
    return (
        dir_x[:, None] * points[0][None, :]
        + dir_y[:, None] * points[1][None, :]
        + dir_z[:, None] * points[2][None, :]
    )


def amplitude_terms(project, weights, shell_q):
    shell_blocks = shell_q.reshape(-1, shell_batch)

    def one_block(shell_block):
        phases = shell_block[:, None, None] * project[None]
        return jnp.stack(
            [
                jnp.sum(weights * jnp.cos(phases), axis=-1),
                jnp.sum(weights * jnp.sin(phases), axis=-1),
            ]
        )

    result = lax.map(one_block, shell_blocks)
    return jnp.transpose(result, (1, 0, 2, 3)).reshape(2, -1, project.shape[0])


def shell_intensity(amplitude):
    return jnp.mean(amplitude[0] * amplitude[0] + amplitude[1] * amplitude[1], axis=-1)


def scale_grad(amplitude, intensity, precision, intensity_exp, total_terms):
    coef_shell = 2.0 * precision * (intensity - intensity_exp) / total_terms
    return coef_shell[None, :, None] * amplitude


def restraint_forces(project, weights, shell_q, weight_grad, dir_x, dir_y, dir_z):
    shell_blocks = shell_q.reshape(-1, shell_batch)
    grad_real = weight_grad[0].reshape(-1, shell_batch, project.shape[0])
    grad_imag = weight_grad[1].reshape(-1, shell_batch, project.shape[0])

    def add_block(running, pieces):
        shell_block, block_real, block_imag = pieces
        phases = shell_block[:, None, None] * project[None]
        block_term = jnp.sum(
            shell_block[:, None, None]
            * (block_imag[:, :, None] * jnp.cos(phases) - block_real[:, :, None] * jnp.sin(phases)),
            axis=0,
        )
        return (running + block_term, None)

    running, unused = lax.scan(
        add_block, jnp.zeros(project.shape, jnp.float32), (shell_blocks, grad_real, grad_imag)
    )
    return jnp.stack(
        [
            -weights * jnp.sum(dir_x[:, None] * running, axis=0),
            -weights * jnp.sum(dir_y[:, None] * running, axis=0),
            -weights * jnp.sum(dir_z[:, None] * running, axis=0),
        ]
    )


def pair_group(own_rows, near_rows, coupling):
    delta_list = [
        own_rows[component][:, :, None] - near_rows[component][:, None, :] for component in range(3)
    ]
    distance = (
        delta_list[0] * delta_list[0]
        + delta_list[1] * delta_list[1]
        + delta_list[2] * delta_list[2]
    )
    pair_weight = (
        coupling
        * own_rows[3][:, :, None]
        * near_rows[3][:, None, :]
        * jnp.exp(-HALF_INVERSE * distance)
    )
    return jnp.stack([jnp.sum(pair_weight * delta, axis=-1) for delta in delta_list])


def pair_forces(own_blocks, ext_blocks, tile_list):
    block_count, neighbours = tile_list.shape
    block_width = own_blocks.shape[2]
    group_size = min(group_limit, block_count)
    coupling = PAIR_STRENGTH / math.sqrt(neighbours * block_width)
    nearby = jnp.take(ext_blocks, tile_list.reshape(-1), axis=1).reshape(
        4, block_count // group_size, group_size, neighbours * block_width
    )
    grouped = own_blocks.reshape(4, block_count // group_size, group_size, block_width)

    def one_group(pieces):
        return pair_group(pieces[0], pieces[1], coupling)

    result = lax.map(one_group, (jnp.moveaxis(grouped, 1, 0), jnp.moveaxis(nearby, 1, 0)))
    return jnp.moveaxis(result, 0, 1).reshape(3, -1)


def shards(
    positions,
    velocities,
    strength,
    inv_mass,
    tile_lists,
    solute_index,
    scatter_weight,
    intensity_exp,
    precision,
):
    coords_now = positions[0]
    speed_now = velocities[0]
    charge = strength[0]
    inverse = inv_mass[0]
    solute_slots = solute_index[0]
    weights = scatter_weight[0]
    atom_dev = coords_now.shape[1]
    rim_width = atom_dev // 2
    block_width = 128
    replica_count = lax.axis_size("rep")
    scale_norm = 1.0 / math.sqrt(lax.axis_size("sp") * solute_slots.shape[0])
    dir_x, dir_y, dir_z = directions(M)
    shell_q = shell_values(intensity_exp.shape[0])
    mass_here = inverse[solute_slots]
    for outer_step in range(OUTER):
        points = jnp.take(coords_now, solute_slots, axis=1)
        project = projection(points, dir_x, dir_y, dir_z)
        partial_value = amplitude_terms(project, weights, shell_q) * scale_norm
        amplitude = lax.psum(partial_value, "sp")
        intensity = lax.psum(shell_intensity(amplitude), "rep") / replica_count
        weight_grad = scale_grad(amplitude, intensity, precision, intensity_exp, M)
        saxs_kick = restraint_forces(project, weights, shell_q, weight_grad, dir_x, dir_y, dir_z)
        for inner_step in range(INNER):
            tile_list = tile_lists[0, outer_step * INNER + inner_step]
            rows_all = jnp.concatenate([coords_now, charge[None, :]], axis=0)
            extended = extended_2(rows_all, (("sp", 1),), rim_width)
            own_blocks = rows_all.reshape(4, atom_dev // block_width, block_width)
            ext_blocks = extended.reshape(4, extended.shape[1] // block_width, block_width)
            pair_push = pair_forces(own_blocks, ext_blocks, tile_list)
            speed_now = speed_now + TIME_STEP * inverse[None, :] * pair_push
            coords_now = coords_now + TIME_STEP * speed_now
        impulse = INNER * TIME_STEP * mass_here[None, :] * saxs_kick
        speed_now = speed_now.at[:, solute_slots].add(impulse)
    return (coords_now[None], speed_now[None])


def solution(mesh):
    in_specs = (
        P("rep", None, "sp"),
        P("rep", None, "sp"),
        P("rep", "sp"),
        P("rep", "sp"),
        P("rep", None, "sp", None),
        P("rep", "sp"),
        P("rep", "sp"),
        P(),
        P(),
    )
    out_specs = (P("rep", None, "sp"), P("rep", None, "sp"))
    return jax.shard_map(shards, mesh=mesh, in_specs=in_specs, out_specs=out_specs, check_vma=False)
```

profile of v0, /device:TPU:24, one launch (start us, length us, event | category | flops | bytes accessed | tf_op | source)
XLA Modules:
  0.0 899.1 jit_solution(11121404440708950667)
XLA Ops:
  74.0 16.2 %while.85 = (s32[]{:T(128)}, f32[8,3,8,128]{3,2,1,0:T(8,128)S(1)}, f32[8,4,8,128]{3,2,1,0:T(8,128)S(1)}, f32[8,4,8,512]{3,2,0,1:T(8,128)S(1)}, s32[]{:T(128)}, /*index=5*/s32[]{:T(128)}, s32[]{}, s32[]{}, s32[]{}) while((s32[]{:T(128)}, f32[8,3,8,128]{3,2,1,0:T(8,128)S(1)}, f32[8,4,8,128]{3,2,1,0:T(8,128)S(1)}, ...), condition=%wide.region_9.11_spmd, body=%wide.region_5.10_spmd.sunk | while | flops 8916997 | bytes 413849 | solution.py:137
  107.9 150.7 %while.89 = (s32[]{:T(128)}, f32[6,2,8,784]{3,2,0,1:T(8,128)S(1)}, f32[1,256]{1,0:T(1,128)S(1)}, f32[6,8]{1,0:T(8,128)S(1)}, f32[256]{0:T(256)S(1)}, /*index=5*/...) while((s32[]{:T(128)}, f32[6,2,8,784]{3,2,0,1:T(8,128)S(1)}, ...), condition=%wide.region_37.40_spmd.clone, body=%wide.region_34.39_spmd.clone.sunk | while | flops 9031682 | bytes 1784213 | solution.py:66
  108.3 24.7 %fusion.158 = (f32[8,784]{1,0:T(8,128)S(1)}, f32[8,784]{1,0:T(8,128)S(1)}) fusion(f32[784,256]{1,0:T(8,128)S(1)} %multiply_add_fusion.13, f32[8]{0:T(128)S(1)} %fusion.157, f32[256]{0:T(256)S(1)} %bitcast.407), kind=kLoop, calls=%fused_computation.132.clone.1 | loop fusion | flops 8015616 | bytes 854048 | tf_op jit(solution)/shard_map/while/body/eval_jaxpr/reduce_sum | solution.py:61
  133.5 24.7 %fusion.158 = (f32[8,784]{1,0:T(8,128)S(1)}, f32[8,784]{1,0:T(8,128)S(1)}) fusion(f32[784,256]{1,0:T(8,128)S(1)} %multiply_add_fusion.13, f32[8]{0:T(128)S(1)} %fusion.157, f32[256]{0:T(256)S(1)} %bitcast.407), kind=kLoop, calls=%fused_computation.132.clone.1 | loop fusion | flops 8015616 | bytes 854048 | tf_op jit(solution)/shard_map/while/body/eval_jaxpr/reduce_sum | solution.py:61
  158.6 24.7 %fusion.158 = (f32[8,784]{1,0:T(8,128)S(1)}, f32[8,784]{1,0:T(8,128)S(1)}) fusion(f32[784,256]{1,0:T(8,128)S(1)} %multiply_add_fusion.13, f32[8]{0:T(128)S(1)} %fusion.157, f32[256]{0:T(256)S(1)} %bitcast.407), kind=kLoop, calls=%fused_computation.132.clone.1 | loop fusion | flops 8015616 | bytes 854048 | tf_op jit(solution)/shard_map/while/body/eval_jaxpr/reduce_sum | solution.py:61
  183.7 24.7 %fusion.158 = (f32[8,784]{1,0:T(8,128)S(1)}, f32[8,784]{1,0:T(8,128)S(1)}) fusion(f32[784,256]{1,0:T(8,128)S(1)} %multiply_add_fusion.13, f32[8]{0:T(128)S(1)} %fusion.157, f32[256]{0:T(256)S(1)} %bitcast.407), kind=kLoop, calls=%fused_computation.132.clone.1 | loop fusion | flops 8015616 | bytes 854048 | tf_op jit(solution)/shard_map/while/body/eval_jaxpr/reduce_sum | solution.py:61
  208.8 24.7 %fusion.158 = (f32[8,784]{1,0:T(8,128)S(1)}, f32[8,784]{1,0:T(8,128)S(1)}) fusion(f32[784,256]{1,0:T(8,128)S(1)} %multiply_add_fusion.13, f32[8]{0:T(128)S(1)} %fusion.157, f32[256]{0:T(256)S(1)} %bitcast.407), kind=kLoop, calls=%fused_computation.132.clone.1 | loop fusion | flops 8015616 | bytes 854048 | tf_op jit(solution)/shard_map/while/body/eval_jaxpr/reduce_sum | solution.py:61
  233.9 24.7 %fusion.158 = (f32[8,784]{1,0:T(8,128)S(1)}, f32[8,784]{1,0:T(8,128)S(1)}) fusion(f32[784,256]{1,0:T(8,128)S(1)} %multiply_add_fusion.13, f32[8]{0:T(128)S(1)} %fusion.157, f32[256]{0:T(256)S(1)} %bitcast.407), kind=kLoop, calls=%fused_computation.132.clone.1 | loop fusion | flops 8015616 | bytes 854048 | tf_op jit(solution)/shard_map/while/body/eval_jaxpr/reduce_sum | solution.py:61
  259.4 150.9 %while.88 = (s32[]{:T(128)}, f32[6,2,8,784]{3,2,0,1:T(8,128)S(1)}, f32[1,256]{1,0:T(1,128)S(1)}, f32[6,8]{1,0:T(8,128)S(1)}, f32[256]{0:T(256)S(1)}, /*index=5*/...) while((s32[]{:T(128)}, f32[6,2,8,784]{3,2,0,1:T(8,128)S(1)}, ...), condition=%wide.region_18.21_spmd.clone, body=%wide.region_15.20_spmd.clone.sunk | while | flops 9031682 | bytes 1784213 | solution.py:66
  260.0 24.7 %fusion.155 = (f32[8,784]{1,0:T(8,128)S(1)}, f32[8,784]{1,0:T(8,128)S(1)}) fusion(f32[784,256]{1,0:T(8,128)S(1)} %multiply_add_fusion.12, f32[8]{0:T(128)S(1)} %fusion.154, f32[256]{0:T(256)S(1)} %bitcast.408), kind=kLoop, calls=%fused_computation.121.clone.1 | loop fusion | flops 8015616 | bytes 854048 | tf_op jit(solution)/shard_map/while/body/eval_jaxpr/reduce_sum | solution.py:61
  285.1 24.7 %fusion.155 = (f32[8,784]{1,0:T(8,128)S(1)}, f32[8,784]{1,0:T(8,128)S(1)}) fusion(f32[784,256]{1,0:T(8,128)S(1)} %multiply_add_fusion.12, f32[8]{0:T(128)S(1)} %fusion.154, f32[256]{0:T(256)S(1)} %bitcast.408), kind=kLoop, calls=%fused_computation.121.clone.1 | loop fusion | flops 8015616 | bytes 854048 | tf_op jit(solution)/shard_map/while/body/eval_jaxpr/reduce_sum | solution.py:61
  310.2 24.7 %fusion.155 = (f32[8,784]{1,0:T(8,128)S(1)}, f32[8,784]{1,0:T(8,128)S(1)}) fusion(f32[784,256]{1,0:T(8,128)S(1)} %multiply_add_fusion.12, f32[8]{0:T(128)S(1)} %fusion.154, f32[256]{0:T(256)S(1)} %bitcast.408), kind=kLoop, calls=%fused_computation.121.clone.1 | loop fusion | flops 8015616 | bytes 854048 | tf_op jit(solution)/shard_map/while/body/eval_jaxpr/reduce_sum | solution.py:61
  335.4 24.7 %fusion.155 = (f32[8,784]{1,0:T(8,128)S(1)}, f32[8,784]{1,0:T(8,128)S(1)}) fusion(f32[784,256]{1,0:T(8,128)S(1)} %multiply_add_fusion.12, f32[8]{0:T(128)S(1)} %fusion.154, f32[256]{0:T(256)S(1)} %bitcast.408), kind=kLoop, calls=%fused_computation.121.clone.1 | loop fusion | flops 8015616 | bytes 854048 | tf_op jit(solution)/shard_map/while/body/eval_jaxpr/reduce_sum | solution.py:61
  360.5 24.7 %fusion.155 = (f32[8,784]{1,0:T(8,128)S(1)}, f32[8,784]{1,0:T(8,128)S(1)}) fusion(f32[784,256]{1,0:T(8,128)S(1)} %multiply_add_fusion.12, f32[8]{0:T(128)S(1)} %fusion.154, f32[256]{0:T(256)S(1)} %bitcast.408), kind=kLoop, calls=%fused_computation.121.clone.1 | loop fusion | flops 8015616 | bytes 854048 | tf_op jit(solution)/shard_map/while/body/eval_jaxpr/reduce_sum | solution.py:61
  385.6 24.7 %fusion.155 = (f32[8,784]{1,0:T(8,128)S(1)}, f32[8,784]{1,0:T(8,128)S(1)}) fusion(f32[784,256]{1,0:T(8,128)S(1)} %multiply_add_fusion.12, f32[8]{0:T(128)S(1)} %fusion.154, f32[256]{0:T(256)S(1)} %bitcast.408), kind=kLoop, calls=%fused_computation.121.clone.1 | loop fusion | flops 8015616 | bytes 854048 | tf_op jit(solution)/shard_map/while/body/eval_jaxpr/reduce_sum | solution.py:61
  450.4 42.0 %all-reduce.4.cloned.1.call-done = (f32[2,48,784]{2,1,0:T(8,128)}, f32[2,48,784]{2,1,0:T(8,128)}) async-done(((f32[2,48,784]{2,1,0:T(8,128)}, f32[2,48,784]{2,1,0:T(8,128)}), (f32[2,48,784]{2,1,0:T(8,128)}, f32[2,48,784]{2,1,0:T(8,128)})) %all-reduce.4.cloned.1.call-update) | async-done | bytes 602128 | tf_op jit(solution)/shard_map/psum | solution.py:170
  494.7 33.4 %all-reduce = (f32[48]{0:T(128)S(1)}, f32[48]{0:T(128)S(1)}) all-reduce(f32[48]{0:T(128)S(1)} %broadcast_multiply_fusion.5, f32[48]{0:T(128)S(1)} %broadcast_multiply_fusion.4), channel_id=1, replica_groups=mesh['rep'=16,'sp'=8] {'rep'}, use_global_device_ids=true, to_apply=%region_21.24 | all-reduce | flops 96 | bytes 768 | tf_op jit(solution)/shard_map/psum | solution.py:171
  529.2 146.9 %while.91 = (s32[]{:T(128)}, f32[784,256]{1,0:T(8,128)S(1)}, f32[6,8]{1,0:T(8,128)S(1)}, f32[6,8,784]{2,1,0:T(8,128)S(1)}, f32[6,8,784]{2,1,0:T(8,128)S(1)}, /*i...) while((s32[]{:T(128)}, f32[784,256]{1,0:T(8,128)S(1)}, ...), condition=%wide.region_43.46_spmd.clone, body=%wide.region_41.45_spmd.clone.sunk | while | flops 10838019 | bytes 4980143 | solution.py:94
  529.6 23.8 %fusion.163 = f32[784,256]{1,0:T(8,128)S(1)} fusion(f32[8,784]{1,0:T(8,128)S(1)} %get-tuple-element.1134, f32[784,256]{1,0:T(8,128)S(1)} %multiply_add_fusion.15, f32[8,784]{1,0:T(8,128)S(1)} %get-tuple-element.1135, f32[8]{0:T(128)S(1)} %fusion.162), kind=kLoop, calls=%fused_computation.158.clone.1 | loop fusion | flops 9433088 | bytes 1655840 | tf_op jit(solution)/shard_map/while/body/eval_jaxpr/reduce_sum | solution.py:87
  554.1 23.8 %fusion.163 = f32[784,256]{1,0:T(8,128)S(1)} fusion(f32[8,784]{1,0:T(8,128)S(1)} %get-tuple-element.1134, f32[784,256]{1,0:T(8,128)S(1)} %multiply_add_fusion.15, f32[8,784]{1,0:T(8,128)S(1)} %get-tuple-element.1135, f32[8]{0:T(128)S(1)} %fusion.162), kind=kLoop, calls=%fused_computation.158.clone.1 | loop fusion | flops 9433088 | bytes 1655840 | tf_op jit(solution)/shard_map/while/body/eval_jaxpr/reduce_sum | solution.py:87
  578.6 23.8 %fusion.163 = f32[784,256]{1,0:T(8,128)S(1)} fusion(f32[8,784]{1,0:T(8,128)S(1)} %get-tuple-element.1134, f32[784,256]{1,0:T(8,128)S(1)} %multiply_add_fusion.15, f32[8,784]{1,0:T(8,128)S(1)} %get-tuple-element.1135, f32[8]{0:T(128)S(1)} %fusion.162), kind=kLoop, calls=%fused_computation.158.clone.1 | loop fusion | flops 9433088 | bytes 1655840 | tf_op jit(solution)/shard_map/while/body/eval_jaxpr/reduce_sum | solution.py:87
  603.1 23.8 %fusion.163 = f32[784,256]{1,0:T(8,128)S(1)} fusion(f32[8,784]{1,0:T(8,128)S(1)} %get-tuple-element.1134, f32[784,256]{1,0:T(8,128)S(1)} %multiply_add_fusion.15, f32[8,784]{1,0:T(8,128)S(1)} %get-tuple-element.1135, f32[8]{0:T(128)S(1)} %fusion.162), kind=kLoop, calls=%fused_computation.158.clone.1 | loop fusion | flops 9433088 | bytes 1655840 | tf_op jit(solution)/shard_map/while/body/eval_jaxpr/reduce_sum | solution.py:87
  627.5 23.8 %fusion.163 = f32[784,256]{1,0:T(8,128)S(1)} fusion(f32[8,784]{1,0:T(8,128)S(1)} %get-tuple-element.1134, f32[784,256]{1,0:T(8,128)S(1)} %multiply_add_fusion.15, f32[8,784]{1,0:T(8,128)S(1)} %get-tuple-element.1135, f32[8]{0:T(128)S(1)} %fusion.162), kind=kLoop, calls=%fused_computation.158.clone.1 | loop fusion | flops 9433088 | bytes 1655840 | tf_op jit(solution)/shard_map/while/body/eval_jaxpr/reduce_sum | solution.py:87
  652.0 23.8 %fusion.163 = f32[784,256]{1,0:T(8,128)S(1)} fusion(f32[8,784]{1,0:T(8,128)S(1)} %get-tuple-element.1134, f32[784,256]{1,0:T(8,128)S(1)} %multiply_add_fusion.15, f32[8,784]{1,0:T(8,128)S(1)} %get-tuple-element.1135, f32[8]{0:T(128)S(1)} %fusion.162), kind=kLoop, calls=%fused_computation.158.clone.1 | loop fusion | flops 9433088 | bytes 1655840 | tf_op jit(solution)/shard_map/while/body/eval_jaxpr/reduce_sum | solution.py:87
  676.2 146.9 %while.90 = (s32[]{:T(128)}, f32[784,256]{1,0:T(8,128)S(1)}, f32[6,8]{1,0:T(8,128)S(1)}, f32[6,8,784]{2,1,0:T(8,128)S(1)}, f32[6,8,784]{2,1,0:T(8,128)S(1)}, /*i...) while((s32[]{:T(128)}, f32[784,256]{1,0:T(8,128)S(1)}, ...), condition=%wide.region_24.27_spmd.clone, body=%wide.region_22.26_spmd.clone.sunk | while | flops 10838019 | bytes 4980143 | solution.py:94
  676.6 23.8 %fusion.161 = f32[784,256]{1,0:T(8,128)S(1)} fusion(f32[8,784]{1,0:T(8,128)S(1)} %get-tuple-element.1121, f32[784,256]{1,0:T(8,128)S(1)} %multiply_add_fusion.14, f32[8,784]{1,0:T(8,128)S(1)} %get-tuple-element.1122, f32[8]{0:T(128)S(1)} %fusion.160), kind=kLoop, calls=%fused_computation.145.clone.1 | loop fusion | flops 9433088 | bytes 1655840 | tf_op jit(solution)/shard_map/while/body/eval_jaxpr/reduce_sum | solution.py:87
  701.1 23.8 %fusion.161 = f32[784,256]{1,0:T(8,128)S(1)} fusion(f32[8,784]{1,0:T(8,128)S(1)} %get-tuple-element.1121, f32[784,256]{1,0:T(8,128)S(1)} %multiply_add_fusion.14, f32[8,784]{1,0:T(8,128)S(1)} %get-tuple-element.1122, f32[8]{0:T(128)S(1)} %fusion.160), kind=kLoop, calls=%fused_computation.145.clone.1 | loop fusion | flops 9433088 | bytes 1655840 | tf_op jit(solution)/shard_map/while/body/eval_jaxpr/reduce_sum | solution.py:87
  725.6 23.8 %fusion.161 = f32[784,256]{1,0:T(8,128)S(1)} fusion(f32[8,784]{1,0:T(8,128)S(1)} %get-tuple-element.1121, f32[784,256]{1,0:T(8,128)S(1)} %multiply_add_fusion.14, f32[8,784]{1,0:T(8,128)S(1)} %get-tuple-element.1122, f32[8]{0:T(128)S(1)} %fusion.160), kind=kLoop, calls=%fused_computation.145.clone.1 | loop fusion | flops 9433088 | bytes 1655840 | tf_op jit(solution)/shard_map/while/body/eval_jaxpr/reduce_sum | solution.py:87
  750.1 23.8 %fusion.161 = f32[784,256]{1,0:T(8,128)S(1)} fusion(f32[8,784]{1,0:T(8,128)S(1)} %get-tuple-element.1121, f32[784,256]{1,0:T(8,128)S(1)} %multiply_add_fusion.14, f32[8,784]{1,0:T(8,128)S(1)} %get-tuple-element.1122, f32[8]{0:T(128)S(1)} %fusion.160), kind=kLoop, calls=%fused_computation.145.clone.1 | loop fusion | flops 9433088 | bytes 1655840 | tf_op jit(solution)/shard_map/while/body/eval_jaxpr/reduce_sum | solution.py:87
  774.6 23.8 %fusion.161 = f32[784,256]{1,0:T(8,128)S(1)} fusion(f32[8,784]{1,0:T(8,128)S(1)} %get-tuple-element.1121, f32[784,256]{1,0:T(8,128)S(1)} %multiply_add_fusion.14, f32[8,784]{1,0:T(8,128)S(1)} %get-tuple-element.1122, f32[8]{0:T(128)S(1)} %fusion.160), kind=kLoop, calls=%fused_computation.145.clone.1 | loop fusion | flops 9433088 | bytes 1655840 | tf_op jit(solution)/shard_map/while/body/eval_jaxpr/reduce_sum | solution.py:87
  799.0 23.8 %fusion.161 = f32[784,256]{1,0:T(8,128)S(1)} fusion(f32[8,784]{1,0:T(8,128)S(1)} %get-tuple-element.1121, f32[784,256]{1,0:T(8,128)S(1)} %multiply_add_fusion.14, f32[8,784]{1,0:T(8,128)S(1)} %get-tuple-element.1122, f32[8]{0:T(128)S(1)} %fusion.160), kind=kLoop, calls=%fused_computation.145.clone.1 | loop fusion | flops 9433088 | bytes 1655840 | tf_op jit(solution)/shard_map/while/body/eval_jaxpr/reduce_sum | solution.py:87
  852.7 16.2 %while.87 = (s32[]{:T(128)}, f32[8,3,8,128]{3,2,1,0:T(8,128)S(1)}, f32[8,4,8,128]{3,2,1,0:T(8,128)S(1)}, f32[8,4,8,512]{3,2,0,1:T(8,128)S(1)}, s32[]{:T(128)}, /*index=5*/s32[]{:T(128)}, s32[]{}, s32[]{}, s32[]{}) while((s32[]{:T(128)}, f32[8,3,8,128]{3,2,1,0:T(8,128)S(1)}, f32[8,4,8,128]{3,2,1,0:T(8,128)S(1)}, ...), condition=%wide.region_33.36_spmd, body=%wide.region_29.35_spmd.sunk | while | flops 8916997 | bytes 413849 | solution.py:137
  (402 shorter events, 256.1 us)
Async XLA Ops:
  7.2 6.4 copy-start.1
  7.2 12.3 %copy-start.5 = (s32[1,4,64,4]{2,3,1,0:T(4,128)S(1)}, s32[1,4,64,4]{2,3,1,0:T(4,128)}, u32[]{:S(2)}) copy-start(s32[1,4,64,4]{2,3,1,0:T(4,128)} %param.33) | copy-start | bytes 12292
  7.2 12.8 %copy-start.6 = (s32[1,256]{1,0:T(1,128)S(1)}, s32[1,256]{1,0:T(1,128)}, u32[]{:S(2)}) copy-start(s32[1,256]{1,0:T(1,128)} %param.34) | copy-start | bytes 3076
  7.2 13.4 %copy-start = (f32[1,8192]{1,0:T(1,128)S(1)}, f32[1,8192]{1,0:T(1,128)}, u32[]{:S(2)}) copy-start(f32[1,8192]{1,0:T(1,128)} %param.32) | copy-start | bytes 98308
  7.2 13.5 %copy-start.4 = (f32[1,3,8192]{2,0,1:T(1,128)S(1)}, f32[1,3,8192]{2,0,1:T(1,128)}, u32[]{:S(2)}) copy-start(f32[1,3,8192]{2,0,1:T(1,128)} %param.30) | copy-start | bytes 294916
  7.2 485.2 %all-reduce.4.cloned.1.call-start = ((), (), s32[]{:S(2)}) async-start(), calls=%async_computation | async-start | bytes 1376256 | tf_op jit(solution)/shard_map/psum | solution.py:170
  10.7 17.3 %copy-start.3 = (f32[1,3,8192]{2,0,1:T(1,128)S(1)}, f32[1,3,8192]{2,0,1:T(1,128)}, u32[]{:S(2)}) copy-start(f32[1,3,8192]{2,0,1:T(1,128)} %param.29) | copy-start | bytes 294916
  13.6 14.4 %collective-permute-start = (f32[4,4096]{1,0:T(4,128)S(1)}, f32[4,4096]{1,0:T(4,128)S(1)}, u32[]{:S(2)}, u32[]{:S(2)}) collective-permute-start(f32[4,4096]{1,0:T(4,128)S(1)} %get-tuple-element.653), channel_id=1, source_target_pairs={{0,1},{1,2},{2,3},{3,4},{4,5},{5,6},{6,7},{8,9},{9,10},{10,11},{11... | collective-permute-start | bytes 196616 | tf_op jit(solution)/shard_map/ppermute | solution.py:25
  17.1 10.9 %collective-permute-start.1 = (f32[4,4096]{1,0:T(4,128)S(1)}, f32[4,4096]{1,0:T(4,128)S(1)}, u32[]{:S(2)}, u32[]{:S(2)}) collective-permute-start(f32[4,4096]{1,0:T(4,128)S(1)} %get-tuple-element.654), channel_id=1, source_target_pairs={{1,0},{2,1},{3,2},{4,3},{5,4},{6,5},{7,6},{9,8},{10,9},{11,10},{12... | collective-permute-start | bytes 196616 | tf_op jit(solution)/shard_map/ppermute | solution.py:27
  58.5 8.1 collective-permute-start.2
  64.1 8.3 collective-permute-start.3
  101.4 6.5 copy-start.7
  411.1 6.1 collective-permute-start.4
  413.0 8.3 collective-permute-start.5
  441.7 86.4 %copy-start.8 = (f32[48]{0:T(128)S(1)}, f32[48]{0:T(128)}, u32[]{:S(2)}) copy-start(f32[48]{0:T(128)} %param.36) | copy-start | bytes 580
  441.7 86.4 %copy-start.9 = (f32[48]{0:T(128)S(1)}, f32[48]{0:T(128)}, u32[]{:S(2)}) copy-start(f32[48]{0:T(128)} %param.37) | copy-start | bytes 580
  529.2 146.9 %copy-start.2 = (f32[2,48,784]{2,1,0:T(8,128)S(1)}, f32[2,48,784]{2,1,0:T(8,128)}, u32[]{:S(2)}) copy-start(f32[2,48,784]{2,1,0:T(8,128)} %get-tuple-element.603) | copy-start | bytes 903172
  838.4 6.7 collective-permute-start.6
  842.8 8.3 collective-permute-start.7
Sparse Core Ops, SparseCore 0:
  417.1 75.2 all-reduce.3
where the time goes:
time: 904 us; the launch traced here: 899 us
  other arithmetic  713 us (79%)
  waiting for transfers between devices  58.1 us (6%)
  local copies, waits for them, and re-layouts  49.9 us (6%)
  blocking collectives  33.4 us (4%)
  starting transfers between devices  26.3 us (3%)
  between operations  15.1 us (2%)
    reduce_sum x12, other arithmetic, one_block(): jnp.sum(weights * jnp.cos(phases), axis=-1)  296 us
    reduce_sum x12, other arithmetic, add_block(): jnp.sum(shell_block[:, None, None] * (block_imag[:, :, None] * jnp.cos(ph...  286 us
    reduce_sum x32, other arithmetic, pair_group(): jnp.sum(pair_weight * delta, axis=-1)  61.6 us
    psum x1, waiting for transfers between devices, shards(): amplitude = lax.psum(partial_value, 'sp')  42 us
    psum x1, blocking collectives, shards(): intensity = lax.psum(shell_intensity(amplitude), 'rep') / replica_count  33.4 us
    add x3, other arithmetic, shards(): coords_now = coords_now + TIME_STEP * speed_now  21.4 us
  transfers between devices with their start and end apart: 9, of which 5 were waited for; matrix products, arithmetic and copies ran while one was open for 4% of the time, Pallas kernels for 0%

commit v1 on v0

--- a/solution.py
+++ b/solution.py
@@ -167,7 +167,7 @@
         points = jnp.take(coords_now, solute_slots, axis=1)
         project = projection(points, dir_x, dir_y, dir_z)
         partial_value = amplitude_terms(project, weights, shell_q) * scale_norm
-        amplitude = lax.psum(partial_value, "sp")
+        amplitude = jnp.sum(lax.all_gather(partial_value, "sp"), axis=0)
         intensity = lax.psum(shell_intensity(amplitude), "rep") / replica_count
         weight_grad = scale_grad(amplitude, intensity, precision, intensity_exp, M)
         saxs_kick = restraint_forces(project, weights, shell_q, weight_grad, dir_x, dir_y, dir_z)

time: 904 us -> 872 us (0.965)
  waiting for transfers between devices: 58.1 us -> 23.2 us
    psum x1 -> x0, waiting for transfers between devices: 42 us -> none  [shards(): amplitude = lax.psum(partial_value, 'sp')]
    all_gather x0 -> x2, waiting for transfers between devices: none -> 11.4 us  [shards(): amplitude = jnp.sum(lax.all_gather(partial_value, 'sp'), axis=0)]
  transfers between devices with their start and end apart: 9 -> 10, of which waited for: 5 -> 3; matrix products, arithmetic and copies ran while one was open for 4% -> 22% of each run, Pallas kernels for 0% -> 0%
where the time goes in v1:
time: 872 us; the launch traced here: 867 us
  other arithmetic  714 us (82%)
  local copies, waits for them, and re-layouts  50.6 us (6%)
  blocking collectives  34.5 us (4%)
  starting transfers between devices  26.1 us (3%)
  waiting for transfers between devices  23.2 us (3%)
  between operations  15.1 us (2%)
    reduce_sum x12, other arithmetic, one_block(): jnp.sum(weights * jnp.cos(phases), axis=-1)  296 us
    reduce_sum x12, other arithmetic, add_block(): jnp.sum(shell_block[:, None, None] * (block_imag[:, :, None] * jnp.cos(ph...  286 us
    reduce_sum x32, other arithmetic, pair_group(): jnp.sum(pair_weight * delta, axis=-1)  61.7 us
    psum x1, blocking collectives, shards(): intensity = lax.psum(shell_intensity(amplitude), 'rep') / replica_count  34.5 us
    add x3, other arithmetic, shards(): coords_now = coords_now + TIME_STEP * speed_now  21.4 us
  transfers between devices with their start and end apart: 10, of which 3 were waited for; matrix products, arithmetic and copies ran while one was open for 22% of the time, Pallas kernels for 0%

profile of v1, /device:TPU:24, one launch (start us, length us, event | category | flops | bytes accessed | tf_op | source)
XLA Modules:
  0.0 866.7 jit_solution(3918767461867138497)
XLA Ops:
  74.6 16.2 %while.85 = (s32[]{:T(128)}, f32[8,3,8,128]{3,2,1,0:T(8,128)S(1)}, f32[8,4,8,128]{3,2,1,0:T(8,128)S(1)}, f32[8,4,8,512]{3,2,0,1:T(8,128)S(1)}, s32[]{:T(128)}, /*index=5*/s32[]{:T(128)}, s32[]{}, s32[]{}, s32[]{}) while((s32[]{:T(128)}, f32[8,3,8,128]{3,2,1,0:T(8,128)S(1)}, f32[8,4,8,128]{3,2,1,0:T(8,128)S(1)}, ...), condition=%wide.region_9.11_spmd, body=%wide.region_5.10_spmd.sunk | while | flops 8916997 | bytes 413849 | solution.py:137
  108.6 150.7 %while.89 = (s32[]{:T(128)}, f32[6,2,8,784]{3,2,0,1:T(8,128)S(1)}, f32[1,256]{1,0:T(1,128)S(1)}, f32[6,8]{1,0:T(8,128)S(1)}, f32[256]{0:T(256)S(1)}, /*index=5*/...) while((s32[]{:T(128)}, f32[6,2,8,784]{3,2,0,1:T(8,128)S(1)}, ...), condition=%wide.region_37.40_spmd.clone, body=%wide.region_34.39_spmd.clone.sunk | while | flops 9031682 | bytes 1784213 | solution.py:66
  109.0 24.7 %fusion.158 = (f32[8,784]{1,0:T(8,128)S(1)}, f32[8,784]{1,0:T(8,128)S(1)}) fusion(f32[784,256]{1,0:T(8,128)S(1)} %multiply_add_fusion.13, f32[8]{0:T(128)S(1)} %fusion.157, f32[256]{0:T(256)S(1)} %bitcast.407), kind=kLoop, calls=%fused_computation.132.clone.1 | loop fusion | flops 8015616 | bytes 854048 | tf_op jit(solution)/shard_map/while/body/eval_jaxpr/reduce_sum | solution.py:61
  134.1 24.7 %fusion.158 = (f32[8,784]{1,0:T(8,128)S(1)}, f32[8,784]{1,0:T(8,128)S(1)}) fusion(f32[784,256]{1,0:T(8,128)S(1)} %multiply_add_fusion.13, f32[8]{0:T(128)S(1)} %fusion.157, f32[256]{0:T(256)S(1)} %bitcast.407), kind=kLoop, calls=%fused_computation.132.clone.1 | loop fusion | flops 8015616 | bytes 854048 | tf_op jit(solution)/shard_map/while/body/eval_jaxpr/reduce_sum | solution.py:61
  159.2 24.7 %fusion.158 = (f32[8,784]{1,0:T(8,128)S(1)}, f32[8,784]{1,0:T(8,128)S(1)}) fusion(f32[784,256]{1,0:T(8,128)S(1)} %multiply_add_fusion.13, f32[8]{0:T(128)S(1)} %fusion.157, f32[256]{0:T(256)S(1)} %bitcast.407), kind=kLoop, calls=%fused_computation.132.clone.1 | loop fusion | flops 8015616 | bytes 854048 | tf_op jit(solution)/shard_map/while/body/eval_jaxpr/reduce_sum | solution.py:61
  184.3 24.7 %fusion.158 = (f32[8,784]{1,0:T(8,128)S(1)}, f32[8,784]{1,0:T(8,128)S(1)}) fusion(f32[784,256]{1,0:T(8,128)S(1)} %multiply_add_fusion.13, f32[8]{0:T(128)S(1)} %fusion.157, f32[256]{0:T(256)S(1)} %bitcast.407), kind=kLoop, calls=%fused_computation.132.clone.1 | loop fusion | flops 8015616 | bytes 854048 | tf_op jit(solution)/shard_map/while/body/eval_jaxpr/reduce_sum | solution.py:61
  209.4 24.7 %fusion.158 = (f32[8,784]{1,0:T(8,128)S(1)}, f32[8,784]{1,0:T(8,128)S(1)}) fusion(f32[784,256]{1,0:T(8,128)S(1)} %multiply_add_fusion.13, f32[8]{0:T(128)S(1)} %fusion.157, f32[256]{0:T(256)S(1)} %bitcast.407), kind=kLoop, calls=%fused_computation.132.clone.1 | loop fusion | flops 8015616 | bytes 854048 | tf_op jit(solution)/shard_map/while/body/eval_jaxpr/reduce_sum | solution.py:61
  234.6 24.7 %fusion.158 = (f32[8,784]{1,0:T(8,128)S(1)}, f32[8,784]{1,0:T(8,128)S(1)}) fusion(f32[784,256]{1,0:T(8,128)S(1)} %multiply_add_fusion.13, f32[8]{0:T(128)S(1)} %fusion.157, f32[256]{0:T(256)S(1)} %bitcast.407), kind=kLoop, calls=%fused_computation.132.clone.1 | loop fusion | flops 8015616 | bytes 854048 | tf_op jit(solution)/shard_map/while/body/eval_jaxpr/reduce_sum | solution.py:61
  266.2 150.7 %while.88 = (s32[]{:T(128)}, f32[6,2,8,784]{3,2,0,1:T(8,128)S(1)}, f32[1,256]{1,0:T(1,128)S(1)}, f32[6,8]{1,0:T(8,128)S(1)}, f32[256]{0:T(256)S(1)}, /*index=5*/...) while((s32[]{:T(128)}, f32[6,2,8,784]{3,2,0,1:T(8,128)S(1)}, ...), condition=%wide.region_18.21_spmd.clone, body=%wide.region_15.20_spmd.clone.sunk | while | flops 9031682 | bytes 1784213 | solution.py:66
  266.6 24.7 %fusion.155 = (f32[8,784]{1,0:T(8,128)S(1)}, f32[8,784]{1,0:T(8,128)S(1)}) fusion(f32[784,256]{1,0:T(8,128)S(1)} %multiply_add_fusion.12, f32[8]{0:T(128)S(1)} %fusion.154, f32[256]{0:T(256)S(1)} %bitcast.408), kind=kLoop, calls=%fused_computation.121.clone.1 | loop fusion | flops 8015616 | bytes 854048 | tf_op jit(solution)/shard_map/while/body/eval_jaxpr/reduce_sum | solution.py:61
  291.7 24.7 %fusion.155 = (f32[8,784]{1,0:T(8,128)S(1)}, f32[8,784]{1,0:T(8,128)S(1)}) fusion(f32[784,256]{1,0:T(8,128)S(1)} %multiply_add_fusion.12, f32[8]{0:T(128)S(1)} %fusion.154, f32[256]{0:T(256)S(1)} %bitcast.408), kind=kLoop, calls=%fused_computation.121.clone.1 | loop fusion | flops 8015616 | bytes 854048 | tf_op jit(solution)/shard_map/while/body/eval_jaxpr/reduce_sum | solution.py:61
  316.8 24.7 %fusion.155 = (f32[8,784]{1,0:T(8,128)S(1)}, f32[8,784]{1,0:T(8,128)S(1)}) fusion(f32[784,256]{1,0:T(8,128)S(1)} %multiply_add_fusion.12, f32[8]{0:T(128)S(1)} %fusion.154, f32[256]{0:T(256)S(1)} %bitcast.408), kind=kLoop, calls=%fused_computation.121.clone.1 | loop fusion | flops 8015616 | bytes 854048 | tf_op jit(solution)/shard_map/while/body/eval_jaxpr/reduce_sum | solution.py:61
  341.9 24.7 %fusion.155 = (f32[8,784]{1,0:T(8,128)S(1)}, f32[8,784]{1,0:T(8,128)S(1)}) fusion(f32[784,256]{1,0:T(8,128)S(1)} %multiply_add_fusion.12, f32[8]{0:T(128)S(1)} %fusion.154, f32[256]{0:T(256)S(1)} %bitcast.408), kind=kLoop, calls=%fused_computation.121.clone.1 | loop fusion | flops 8015616 | bytes 854048 | tf_op jit(solution)/shard_map/while/body/eval_jaxpr/reduce_sum | solution.py:61
  367.0 24.7 %fusion.155 = (f32[8,784]{1,0:T(8,128)S(1)}, f32[8,784]{1,0:T(8,128)S(1)}) fusion(f32[784,256]{1,0:T(8,128)S(1)} %multiply_add_fusion.12, f32[8]{0:T(128)S(1)} %fusion.154, f32[256]{0:T(256)S(1)} %bitcast.408), kind=kLoop, calls=%fused_computation.121.clone.1 | loop fusion | flops 8015616 | bytes 854048 | tf_op jit(solution)/shard_map/while/body/eval_jaxpr/reduce_sum | solution.py:61
  392.1 24.7 %fusion.155 = (f32[8,784]{1,0:T(8,128)S(1)}, f32[8,784]{1,0:T(8,128)S(1)}) fusion(f32[784,256]{1,0:T(8,128)S(1)} %multiply_add_fusion.12, f32[8]{0:T(128)S(1)} %fusion.154, f32[256]{0:T(256)S(1)} %bitcast.408), kind=kLoop, calls=%fused_computation.121.clone.1 | loop fusion | flops 8015616 | bytes 854048 | tf_op jit(solution)/shard_map/while/body/eval_jaxpr/reduce_sum | solution.py:61
  419.2 16.2 %while.86 = (s32[]{:T(128)}, f32[8,3,8,128]{3,2,1,0:T(8,128)S(1)}, f32[8,4,8,128]{3,2,1,0:T(8,128)S(1)}, f32[8,4,8,512]{3,2,0,1:T(8,128)S(1)}, s32[]{:T(128)}, /*index=5*/s32[]{:T(128)}, s32[]{}, s32[]{}, s32[]{}) while((s32[]{:T(128)}, f32[8,3,8,128]{3,2,1,0:T(8,128)S(1)}, f32[8,4,8,128]{3,2,1,0:T(8,128)S(1)}, ...), condition=%wide.region_14.16_spmd, body=%wide.region_10.15_spmd.sunk | while | flops 8916997 | bytes 413849 | solution.py:137
  462.6 34.5 %all-reduce = (f32[48]{0:T(128)S(1)}, f32[48]{0:T(128)S(1)}) all-reduce(f32[48]{0:T(128)S(1)} %broadcast_multiply_fusion.5, f32[48]{0:T(128)S(1)} %broadcast_multiply_fusion.4), channel_id=1, replica_groups=mesh['rep'=16,'sp'=8] {'rep'}, use_global_device_ids=true, to_apply=%region_21.24 | all-reduce | flops 96 | bytes 768 | tf_op jit(solution)/shard_map/psum | solution.py:171
  497.2 146.9 %while.91 = (s32[]{:T(128)}, f32[784,256]{1,0:T(8,128)S(1)}, f32[6,8]{1,0:T(8,128)S(1)}, f32[6,8,784]{2,1,0:T(8,128)S(1)}, f32[6,8,784]{2,1,0:T(8,128)S(1)}, /*i...) while((s32[]{:T(128)}, f32[784,256]{1,0:T(8,128)S(1)}, ...), condition=%wide.region_43.46_spmd.clone, body=%wide.region_41.45_spmd.clone.sunk | while | flops 10838019 | bytes 4980143 | solution.py:94
  497.6 23.8 %fusion.163 = f32[784,256]{1,0:T(8,128)S(1)} fusion(f32[8,784]{1,0:T(8,128)S(1)} %get-tuple-element.1132, f32[784,256]{1,0:T(8,128)S(1)} %multiply_add_fusion.15, f32[8,784]{1,0:T(8,128)S(1)} %get-tuple-element.1133, f32[8]{0:T(128)S(1)} %fusion.162), kind=kLoop, calls=%fused_computation.158.clone.1 | loop fusion | flops 9433088 | bytes 1655840 | tf_op jit(solution)/shard_map/while/body/eval_jaxpr/reduce_sum | solution.py:87
  522.1 23.8 %fusion.163 = f32[784,256]{1,0:T(8,128)S(1)} fusion(f32[8,784]{1,0:T(8,128)S(1)} %get-tuple-element.1132, f32[784,256]{1,0:T(8,128)S(1)} %multiply_add_fusion.15, f32[8,784]{1,0:T(8,128)S(1)} %get-tuple-element.1133, f32[8]{0:T(128)S(1)} %fusion.162), kind=kLoop, calls=%fused_computation.158.clone.1 | loop fusion | flops 9433088 | bytes 1655840 | tf_op jit(solution)/shard_map/while/body/eval_jaxpr/reduce_sum | solution.py:87
  546.6 23.8 %fusion.163 = f32[784,256]{1,0:T(8,128)S(1)} fusion(f32[8,784]{1,0:T(8,128)S(1)} %get-tuple-element.1132, f32[784,256]{1,0:T(8,128)S(1)} %multiply_add_fusion.15, f32[8,784]{1,0:T(8,128)S(1)} %get-tuple-element.1133, f32[8]{0:T(128)S(1)} %fusion.162), kind=kLoop, calls=%fused_computation.158.clone.1 | loop fusion | flops 9433088 | bytes 1655840 | tf_op jit(solution)/shard_map/while/body/eval_jaxpr/reduce_sum | solution.py:87
  571.1 23.8 %fusion.163 = f32[784,256]{1,0:T(8,128)S(1)} fusion(f32[8,784]{1,0:T(8,128)S(1)} %get-tuple-element.1132, f32[784,256]{1,0:T(8,128)S(1)} %multiply_add_fusion.15, f32[8,784]{1,0:T(8,128)S(1)} %get-tuple-element.1133, f32[8]{0:T(128)S(1)} %fusion.162), kind=kLoop, calls=%fused_computation.158.clone.1 | loop fusion | flops 9433088 | bytes 1655840 | tf_op jit(solution)/shard_map/while/body/eval_jaxpr/reduce_sum | solution.py:87
  595.5 23.8 %fusion.163 = f32[784,256]{1,0:T(8,128)S(1)} fusion(f32[8,784]{1,0:T(8,128)S(1)} %get-tuple-element.1132, f32[784,256]{1,0:T(8,128)S(1)} %multiply_add_fusion.15, f32[8,784]{1,0:T(8,128)S(1)} %get-tuple-element.1133, f32[8]{0:T(128)S(1)} %fusion.162), kind=kLoop, calls=%fused_computation.158.clone.1 | loop fusion | flops 9433088 | bytes 1655840 | tf_op jit(solution)/shard_map/while/body/eval_jaxpr/reduce_sum | solution.py:87
  620.0 23.8 %fusion.163 = f32[784,256]{1,0:T(8,128)S(1)} fusion(f32[8,784]{1,0:T(8,128)S(1)} %get-tuple-element.1132, f32[784,256]{1,0:T(8,128)S(1)} %multiply_add_fusion.15, f32[8,784]{1,0:T(8,128)S(1)} %get-tuple-element.1133, f32[8]{0:T(128)S(1)} %fusion.162), kind=kLoop, calls=%fused_computation.158.clone.1 | loop fusion | flops 9433088 | bytes 1655840 | tf_op jit(solution)/shard_map/while/body/eval_jaxpr/reduce_sum | solution.py:87
  644.2 146.9 %while.90 = (s32[]{:T(128)}, f32[784,256]{1,0:T(8,128)S(1)}, f32[6,8]{1,0:T(8,128)S(1)}, f32[6,8,784]{2,1,0:T(8,128)S(1)}, f32[6,8,784]{2,1,0:T(8,128)S(1)}, /*i...) while((s32[]{:T(128)}, f32[784,256]{1,0:T(8,128)S(1)}, ...), condition=%wide.region_24.27_spmd.clone, body=%wide.region_22.26_spmd.clone.sunk | while | flops 10838019 | bytes 4980143 | solution.py:94
  644.6 23.8 %fusion.161 = f32[784,256]{1,0:T(8,128)S(1)} fusion(f32[8,784]{1,0:T(8,128)S(1)} %get-tuple-element.1119, f32[784,256]{1,0:T(8,128)S(1)} %multiply_add_fusion.14, f32[8,784]{1,0:T(8,128)S(1)} %get-tuple-element.1120, f32[8]{0:T(128)S(1)} %fusion.160), kind=kLoop, calls=%fused_computation.145.clone.1 | loop fusion | flops 9433088 | bytes 1655840 | tf_op jit(solution)/shard_map/while/body/eval_jaxpr/reduce_sum | solution.py:87
  669.1 23.8 %fusion.161 = f32[784,256]{1,0:T(8,128)S(1)} fusion(f32[8,784]{1,0:T(8,128)S(1)} %get-tuple-element.1119, f32[784,256]{1,0:T(8,128)S(1)} %multiply_add_fusion.14, f32[8,784]{1,0:T(8,128)S(1)} %get-tuple-element.1120, f32[8]{0:T(128)S(1)} %fusion.160), kind=kLoop, calls=%fused_computation.145.clone.1 | loop fusion | flops 9433088 | bytes 1655840 | tf_op jit(solution)/shard_map/while/body/eval_jaxpr/reduce_sum | solution.py:87
  693.6 23.8 %fusion.161 = f32[784,256]{1,0:T(8,128)S(1)} fusion(f32[8,784]{1,0:T(8,128)S(1)} %get-tuple-element.1119, f32[784,256]{1,0:T(8,128)S(1)} %multiply_add_fusion.14, f32[8,784]{1,0:T(8,128)S(1)} %get-tuple-element.1120, f32[8]{0:T(128)S(1)} %fusion.160), kind=kLoop, calls=%fused_computation.145.clone.1 | loop fusion | flops 9433088 | bytes 1655840 | tf_op jit(solution)/shard_map/while/body/eval_jaxpr/reduce_sum | solution.py:87
  718.1 23.8 %fusion.161 = f32[784,256]{1,0:T(8,128)S(1)} fusion(f32[8,784]{1,0:T(8,128)S(1)} %get-tuple-element.1119, f32[784,256]{1,0:T(8,128)S(1)} %multiply_add_fusion.14, f32[8,784]{1,0:T(8,128)S(1)} %get-tuple-element.1120, f32[8]{0:T(128)S(1)} %fusion.160), kind=kLoop, calls=%fused_computation.145.clone.1 | loop fusion | flops 9433088 | bytes 1655840 | tf_op jit(solution)/shard_map/while/body/eval_jaxpr/reduce_sum | solution.py:87
  742.5 23.8 %fusion.161 = f32[784,256]{1,0:T(8,128)S(1)} fusion(f32[8,784]{1,0:T(8,128)S(1)} %get-tuple-element.1119, f32[784,256]{1,0:T(8,128)S(1)} %multiply_add_fusion.14, f32[8,784]{1,0:T(8,128)S(1)} %get-tuple-element.1120, f32[8]{0:T(128)S(1)} %fusion.160), kind=kLoop, calls=%fused_computation.145.clone.1 | loop fusion | flops 9433088 | bytes 1655840 | tf_op jit(solution)/shard_map/while/body/eval_jaxpr/reduce_sum | solution.py:87
  767.0 23.8 %fusion.161 = f32[784,256]{1,0:T(8,128)S(1)} fusion(f32[8,784]{1,0:T(8,128)S(1)} %get-tuple-element.1119, f32[784,256]{1,0:T(8,128)S(1)} %multiply_add_fusion.14, f32[8,784]{1,0:T(8,128)S(1)} %get-tuple-element.1120, f32[8]{0:T(128)S(1)} %fusion.160), kind=kLoop, calls=%fused_computation.145.clone.1 | loop fusion | flops 9433088 | bytes 1655840 | tf_op jit(solution)/shard_map/while/body/eval_jaxpr/reduce_sum | solution.py:87
  820.2 16.2 %while.87 = (s32[]{:T(128)}, f32[8,3,8,128]{3,2,1,0:T(8,128)S(1)}, f32[8,4,8,128]{3,2,1,0:T(8,128)S(1)}, f32[8,4,8,512]{3,2,0,1:T(8,128)S(1)}, s32[]{:T(128)}, /*index=5*/s32[]{:T(128)}, s32[]{}, s32[]{}, s32[]{}) while((s32[]{:T(128)}, f32[8,3,8,128]{3,2,1,0:T(8,128)S(1)}, f32[8,4,8,128]{3,2,1,0:T(8,128)S(1)}, ...), condition=%wide.region_33.36_spmd, body=%wide.region_29.35_spmd.sunk | while | flops 8916997 | bytes 413849 | solution.py:137
  (407 shorter events, 248.6 us)
Async XLA Ops:
  7.2 6.4 copy-start.1
  7.2 12.3 %copy-start.5 = (s32[1,4,64,4]{2,3,1,0:T(4,128)S(1)}, s32[1,4,64,4]{2,3,1,0:T(4,128)}, u32[]{:S(2)}) copy-start(s32[1,4,64,4]{2,3,1,0:T(4,128)} %param.33) | copy-start | bytes 12292
  7.2 12.8 %copy-start.6 = (s32[1,256]{1,0:T(1,128)S(1)}, s32[1,256]{1,0:T(1,128)}, u32[]{:S(2)}) copy-start(s32[1,256]{1,0:T(1,128)} %param.34) | copy-start | bytes 3076
  7.2 13.4 %copy-start = (f32[1,8192]{1,0:T(1,128)S(1)}, f32[1,8192]{1,0:T(1,128)}, u32[]{:S(2)}) copy-start(f32[1,8192]{1,0:T(1,128)} %param.32) | copy-start | bytes 98308
  7.2 13.5 %copy-start.4 = (f32[1,3,8192]{2,0,1:T(1,128)S(1)}, f32[1,3,8192]{2,0,1:T(1,128)}, u32[]{:S(2)}) copy-start(f32[1,3,8192]{2,0,1:T(1,128)} %param.30) | copy-start | bytes 294916
  7.2 439.7 %all-gather.5.cloned.1.call-start = ((), (), s32[]{:S(2)}) async-start(), calls=%async_computation.1 | async-start | bytes 3096576 | tf_op jit(solution)/shard_map/all_gather | solution.py:170
  10.7 17.9 %copy-start.2 = (f32[1,3,8192]{2,0,1:T(1,128)S(1)}, f32[1,3,8192]{2,0,1:T(1,128)}, u32[]{:S(2)}) copy-start(f32[1,3,8192]{2,0,1:T(1,128)} %param.29) | copy-start | bytes 294916
  13.6 15.0 %collective-permute-start = (f32[4,4096]{1,0:T(4,128)S(1)}, f32[4,4096]{1,0:T(4,128)S(1)}, u32[]{:S(2)}, u32[]{:S(2)}) collective-permute-start(f32[4,4096]{1,0:T(4,128)S(1)} %get-tuple-element.651), channel_id=1, source_target_pairs={{0,1},{1,2},{2,3},{3,4},{4,5},{5,6},{6,7},{8,9},{9,10},{10,11},{11... | collective-permute-start | bytes 196616 | tf_op jit(solution)/shard_map/ppermute | solution.py:25
  17.1 11.5 %collective-permute-start.1 = (f32[4,4096]{1,0:T(4,128)S(1)}, f32[4,4096]{1,0:T(4,128)S(1)}, u32[]{:S(2)}, u32[]{:S(2)}) collective-permute-start(f32[4,4096]{1,0:T(4,128)S(1)} %get-tuple-element.652), channel_id=1, source_target_pairs={{1,0},{2,1},{3,2},{4,3},{5,4},{6,5},{7,6},{9,8},{10,9},{11,10},{12... | collective-permute-start | bytes 196616 | tf_op jit(solution)/shard_map/ppermute | solution.py:27
  59.1 8.1 collective-permute-start.2
  64.7 8.3 collective-permute-start.3
  102.0 5.9 copy-start.3
  102.0 6.6 copy-start.7
  260.0 200.4 %all-gather.3.cloned.1.call-start = ((), (), s32[]{:S(2)}) async-start(), calls=%async_computation | async-start | bytes 3096576 | tf_op jit(solution)/shard_map/all_gather | solution.py:170
  260.1 157.5 %collective-permute-start.4 = (f32[4,4096]{1,0:T(4,128)S(1)}, f32[4,4096]{1,0:T(4,128)S(1)}, u32[]{:S(2)}, u32[]{:S(2)}) collective-permute-start(f32[4,4096]{1,0:T(4,128)S(1)} %get-tuple-element.647), channel_id=1, source_target_pairs={{0,1},{1,2},{2,3},{3,4},{4,5},{5,6},{6,7},{8,9},{9,10},{10,11},{11... | collective-permute-start | bytes 196616 | tf_op jit(solution)/shard_map/ppermute | solution.py:25
  262.0 155.6 %collective-permute-start.5 = (f32[4,4096]{1,0:T(4,128)S(1)}, f32[4,4096]{1,0:T(4,128)S(1)}, u32[]{:S(2)}, u32[]{:S(2)}) collective-permute-start(f32[4,4096]{1,0:T(4,128)S(1)} %get-tuple-element.648), channel_id=1, source_target_pairs={{1,0},{2,1},{3,2},{4,3},{5,4},{6,5},{7,6},{9,8},{10,9},{11,10},{12... | collective-permute-start | bytes 196616 | tf_op jit(solution)/shard_map/ppermute | solution.py:27
  446.9 50.2 %copy-start.8 = (f32[48]{0:T(128)S(1)}, f32[48]{0:T(128)}, u32[]{:S(2)}) copy-start(f32[48]{0:T(128)} %param.36) | copy-start | bytes 580
  446.9 50.2 %copy-start.9 = (f32[48]{0:T(128)S(1)}, f32[48]{0:T(128)}, u32[]{:S(2)}) copy-start(f32[48]{0:T(128)} %param.37) | copy-start | bytes 580
  806.4 6.3 collective-permute-start.6
  810.4 8.3 collective-permute-start.7
Sparse Core Ops, SparseCore 0:
  260.2 42.6 all-gather.4
  417.7 42.6 all-gather.2
